TPU v7x, 256 devices: a whole 4x4x8 slice. The times are simulated.
256 devices in a mesh: section: 32 (over z_lo, x, core), tensor: 8 (over y, z_hi).
Axes of the slice: x: 4, y: 4, z: 8 (z_hi: 2, z_lo: 4; z = z_hi * 4 + z_lo), core: 2. Of those that a mesh axis runs over, the one named last changes fastest.
Arguments:
- forward_input: bfloat16 [32, 256, 8192], P('section', None, 'tensor'), may hold values from -6 to 6
- saved_last: bfloat16 [32, 256, 8192], P('section', None, 'tensor'), may hold values from -6 to 6
- saved_first: bfloat16 [32, 256, 8192], P('section', None, 'tensor'), may hold values from -6 to 6
- first_cotangent: bfloat16 [32, 256, 8192], P('section', None, 'tensor'), may hold values from -6 to 6
- section_entry: bfloat16 [256, 8192], P(None, 'tensor'), may hold values from -6 to 6
- last_gain: float32 [32, 8192], P('section'), may hold values from 0.1 to 1.9
- last_up: bfloat16 [32, 8192, 1024], P('section', None, 'tensor'), may hold values from -0.0625 to 0.0625
- last_down: bfloat16 [32, 1024, 8192], P('section', 'tensor'), may hold values from -0.1875 to 0.1875
- first_gain: float32 [32, 8192], P('section'), may hold values from 0.1 to 1.9
- first_up: bfloat16 [32, 8192, 1024], P('section', None, 'tensor'), may hold values from -0.0625 to 0.0625
- first_down: bfloat16 [32, 1024, 8192], P('section', 'tensor'), may hold values from -0.1875 to 0.1875
- head_gain: float32 [8192], replicated, may hold values from 0.1 to 1.9
- head_weight: float32 [8192, 4], P('tensor'), may hold values from -0.0625 to 0.0625
- head_bias: float32 [4], replicated, may hold values from -3 to 3
- prompt_length: int32 [1], replicated, may hold values from 8 to 248
- keep_mask: int32 [1, 256], replicated, may hold values 0 or 1
- target_box: int32 [1, 4], replicated, may hold values from 0 to 1000, as said below
Outputs:
- layer_output: bfloat16 [32, 256, 8192], P('section', None, 'tensor')
- input_gradient: bfloat16 [32, 256, 8192], P('section', None, 'tensor')
Inputs may be any that keep to these rules, and one draw needn't show every extreme that they name: `target_box`: each row is a box x1, y1, x2, y2 with x2 - x1 and y2 - y1 at least 100.
All inputs are finite; a program needn't handle non-finite values.
Results may differ from a plain program's by a relative error of at most 0.018.
Values may be sent and summed in bfloat16 or wider, within the bound.
A program may use at most 128 MiB of HBM per device.

v0:
```python
import jax
import jax.numpy as jnp
from jax import lax
from jax.sharding import PartitionSpec as P

epsilon = 1e-06
softness = 4.0
loss_scale = 4096.0


def shifted(value, axis, steps):
    count = lax.axis_size(axis)
    initial, last = (max(0, -steps), min(count, count - steps))
    return lax.ppermute(value, axis, [(source, source + steps) for source in range(initial, last)])


def unit_rows(values):
    values = values.astype(jnp.float32)
    inverse = lax.rsqrt(jnp.mean(values * values, axis=-1, keepdims=True) + epsilon)
    return (values * inverse, inverse)


def column_start(local_width):
    return lax.axis_index("tensor") * local_width


def column_slice(full_rows, local_width):
    return lax.dynamic_slice_in_dim(full_rows, column_start(local_width), local_width, 1)


def gather_columns(local_rows):
    return lax.all_gather(local_rows, "tensor", axis=1, tiled=True)


def reduce_columns(partial_rows):
    return lax.psum_scatter(
        partial_rows.astype(jnp.bfloat16), "tensor", scatter_dimension=1, tiled=True
    ).astype(jnp.float32)


def row_sums(values):
    return lax.psum(values, "tensor")


def layer_core(full_rows, gain_row, up_matrix, down_matrix):
    scaled, inverse = unit_rows(full_rows)
    normed = (scaled * gain_row).astype(jnp.bfloat16)
    activated = jax.nn.silu(jnp.dot(normed, up_matrix, preferred_element_type=jnp.float32)).astype(
        jnp.bfloat16
    )
    return jnp.dot(activated, down_matrix, preferred_element_type=jnp.float32)


def layer_backward(saved_rows, cotangent, gain_row, up_matrix, down_matrix):
    saved_full, cotangent_full = (
        lax.all_gather(saved_rows, "tensor", axis=1, tiled=True),
        lax.all_gather(cotangent, "tensor", axis=1, tiled=True),
    )
    scaled, inverse = unit_rows(saved_full)
    normed = (scaled * gain_row).astype(jnp.bfloat16)
    pre_act = jnp.dot(normed, up_matrix, preferred_element_type=jnp.float32)
    act_grad = lax.dot_general(
        cotangent_full, down_matrix, (((1,), (1,)), ((), ())), preferred_element_type=jnp.float32
    )
    sigmoid_pre = jax.nn.sigmoid(pre_act)
    pre_grad = (act_grad * sigmoid_pre * (1.0 + pre_act * (1.0 - sigmoid_pre))).astype(jnp.bfloat16)
    norm_partial = lax.dot_general(
        pre_grad, up_matrix, (((1,), (1,)), ((), ())), preferred_element_type=jnp.float32
    )
    norm_grad = reduce_columns(norm_partial)
    local_width = cotangent.shape[1]
    full_width = saved_full.shape[1]
    scaled_cols = column_slice(scaled, local_width)
    gain_cols = lax.dynamic_slice_in_dim(gain_row, column_start(local_width), local_width, 0)
    row_total = row_sums(jnp.sum(scaled_cols * gain_cols * norm_grad, axis=1))
    result = cotangent.astype(jnp.float32) + inverse * (
        gain_cols * norm_grad - scaled_cols * row_total[:, None] / full_width
    )
    return result.astype(jnp.bfloat16)


def soft_min(first, second):
    return 0.5 * (
        first + second - jnp.sqrt((first - second) * (first - second) + softness * softness)
    )


def soft_max(first, second):
    return 0.5 * (
        first + second + jnp.sqrt((first - second) * (first - second) + softness * softness)
    )


def soft_relu(difference):
    return 0.5 * (difference + jnp.sqrt(difference * difference + softness * softness))


def box_loss(logits, target_box):
    scaled_box = jax.nn.sigmoid(logits) * 1000.0
    centre_x = scaled_box[:, 0]
    centre_y = scaled_box[:, 1]
    box_width = scaled_box[:, 2]
    box_height = scaled_box[:, 3]
    left_pred = centre_x - 0.5 * box_width
    right_pred = centre_x + 0.5 * box_width
    lower_pred = centre_y - 0.5 * box_height
    upper_pred = centre_y + 0.5 * box_height
    target = target_box.astype(jnp.float32)
    inner_width = soft_relu(soft_min(right_pred, target[:, 2]) - soft_max(left_pred, target[:, 0]))
    inner_height = soft_relu(
        soft_min(upper_pred, target[:, 3]) - soft_max(lower_pred, target[:, 1])
    )
    intersection_area = inner_width * inner_height
    target_area = (target[:, 2] - target[:, 0]) * (target[:, 3] - target[:, 1])
    union_area = box_width * box_height + target_area - intersection_area
    outer_width = soft_max(right_pred, target[:, 2]) - soft_min(left_pred, target[:, 0])
    outer_height = soft_max(upper_pred, target[:, 3]) - soft_min(lower_pred, target[:, 1])
    enclosing = outer_width * outer_height
    return loss_scale * jnp.mean(
        1.0 - intersection_area / union_area + (enclosing - union_area) / enclosing
    )


def head_cotangent(
    final_rows, head_gain, head_weight, head_bias, prompt_length, keep_mask, target_box
):
    row_count = keep_mask.shape[0]
    positions = jnp.arange(keep_mask.shape[1], dtype=jnp.int32)[None, :]
    starts = prompt_length[:, None]
    weights = (positions == starts - 1).astype(jnp.float32) + (positions >= starts).astype(
        jnp.float32
    ) * keep_mask.astype(jnp.float32)
    counts = jnp.sum(weights, axis=1)
    local_width = final_rows.shape[1]
    full_width = local_width * lax.axis_size("tensor")
    tokens = final_rows.astype(jnp.float32).reshape(row_count, keep_mask.shape[1], local_width)
    pooled = (
        jnp.einsum("rt,rtd->rd", weights, tokens, precision=lax.Precision.HIGHEST) / counts[:, None]
    )
    gain_cols = lax.dynamic_slice_in_dim(head_gain, column_start(local_width), local_width, 0)
    logit_part = jnp.dot(pooled * gain_cols, head_weight, precision=lax.Precision.HIGHEST)
    square_part = jnp.sum(pooled * pooled, axis=1, keepdims=True)
    totals = row_sums(jnp.concatenate([logit_part, square_part], axis=1))
    inverse = lax.rsqrt(totals[:, 4] / full_width + epsilon)
    logits = totals[:, :4] * inverse[:, None] + head_bias

    def loss_of(logit_value):
        return box_loss(logit_value, target_box)

    loss_value, pullback = jax.vjp(loss_of, logits)
    logit_grad = pullback(jnp.ones((), jnp.float32))[0]
    scaled_grad = jnp.dot(logit_grad, head_weight.T, precision=lax.Precision.HIGHEST)
    unit_pooled = pooled * inverse[:, None]
    row_total = row_sums(jnp.sum(unit_pooled * gain_cols * scaled_grad, axis=1))
    pooled_grad = inverse[:, None] * (
        gain_cols * scaled_grad - unit_pooled * row_total[:, None] / full_width
    )
    token_grad = (weights / counts[:, None])[:, :, None] * pooled_grad[:, None, :]
    return token_grad.reshape(final_rows.shape[0], local_width).astype(jnp.bfloat16)


def per_device(
    forward_input,
    saved_last,
    saved_first,
    first_cotangent,
    section_entry,
    last_gain,
    last_up,
    last_down,
    first_gain,
    first_up,
    first_down,
    head_gain,
    head_weight,
    head_bias,
    prompt_length,
    keep_mask,
    target_box,
):
    section_index = lax.axis_index("section")
    opening = section_index == 0
    closing = section_index == lax.axis_size("section") - 1
    local_input = forward_input[0]
    gathered_input = gather_columns(local_input)
    last_partial = layer_core(gathered_input, last_gain[0], last_up[0], last_down[0])
    hidden_local = (local_input.astype(jnp.float32) + reduce_columns(last_partial)).astype(
        jnp.bfloat16
    )
    arrived_local = shifted(hidden_local, "section", 1)
    entry_local = jnp.where(opening, section_entry, arrived_local)
    entry_full = gather_columns(entry_local)
    first_partial = layer_core(entry_full, first_gain[0], first_up[0], first_down[0])
    layer_output = (entry_local.astype(jnp.float32) + reduce_columns(first_partial)).astype(
        jnp.bfloat16
    )
    first_grad = layer_backward(
        saved_first[0], first_cotangent[0], first_gain[0], first_up[0], first_down[0]
    )
    returned = shifted(first_grad, "section", -1)
    head_grad = head_cotangent(
        hidden_local, head_gain, head_weight, head_bias, prompt_length, keep_mask, target_box
    )
    cotangent = jnp.where(closing, head_grad, returned)
    saved_rows = jnp.where(closing, local_input, saved_last[0])
    input_gradient = layer_backward(saved_rows, cotangent, last_gain[0], last_up[0], last_down[0])
    return (layer_output[None], input_gradient[None])


def solution(mesh):
    placed = (
        P("section", None, "tensor"),
        P("section", None, "tensor"),
        P("section", None, "tensor"),
        P("section", None, "tensor"),
        P(None, "tensor"),
        P("section", None),
        P("section", None, "tensor"),
        P("section", "tensor", None),
        P("section", None),
        P("section", None, "tensor"),
        P("section", "tensor", None),
        P(),
        P("tensor", None),
        P(),
        P(),
        P(),
        P(),
    )
    return jax.shard_map(
        per_device,
        mesh=mesh,
        in_specs=placed,
        out_specs=(P("section", None, "tensor"), P("section", None, "tensor")),
        check_vma=False,
    )
```

profile of v0, /device:TPU:2, one launch (start us, length us, event | category | flops | bytes accessed | tf_op | source)
XLA Modules:
  0.0 1165.1 jit_solution(11418929649073457624)
XLA Ops:
  7.2 0.7 all-gather.15.cloned.1.call-update
  8.0 0.7 all-gather.17.cloned.1.call-update
  8.7 0.7 all-gather.19.cloned.1.call-update
  9.5 111.2 %all-gather.15.cloned.1.call-done = bf16[1,256,8192]{2,1,0:T(8,128)(2,1)} async-done(((bf16[1,256,1024]{2,1,0:T(8,128)(2,1)}), bf16[1,256,8192]{2,1,0:T(8,128)(2,1)}) %all-gather.15.cloned.1.call-update) | async-done | bytes 4194320 | tf_op jit(solution)/shard_map/all_gather | solution.py:32
  120.7 3.1 fusion.3
  123.8 7.4 convolution_convert_fusion.3
  131.2 0.0 reduce-scatter.9.cloned.1.call-start
  131.3 93.7 %all-gather.17.cloned.1.call-done = bf16[1,256,8192]{2,1,0:T(8,128)(2,1)} async-done(((bf16[1,256,1024]{2,1,0:T(8,128)(2,1)}), bf16[1,256,8192]{2,1,0:T(8,128)(2,1)}) %all-gather.17.cloned.1.call-update) | async-done | bytes 4194320 | tf_op jit(solution)/shard_map/all_gather | solution.py:56
  225.0 3.3 fusion.6
  228.3 0.2 copy-done.2
  228.5 3.0 fusion.8
  231.5 97.9 %all-gather.19.cloned.1.call-done = bf16[1,256,8192]{2,1,0:T(8,128)(2,1)} async-done(((bf16[1,256,1024]{2,1,0:T(8,128)(2,1)}), bf16[1,256,8192]{2,1,0:T(8,128)(2,1)}) %all-gather.19.cloned.1.call-update) | async-done | bytes 4194320 | tf_op jit(solution)/shard_map/all_gather | solution.py:57
  329.4 9.9 convolution_convert_fusion.1
  339.3 0.0 all-gather.21.cloned.1.call-start
  339.4 1.1 copy-done.3
  340.5 0.3 copy-done.8
  340.7 0.8 broadcast_select_fusion
  341.6 0.0 all-gather.13.cloned.1.call-start
  342.3 0.7 fusion.139
  345.5 0.6 fusion.137
  346.2 108.6 %reduce-scatter.5.cloned.1.call-done = bf16[256,1024]{1,0:T(8,128)(2,1)} async-done(((bf16[256,8192]{1,0:T(8,128)(2,1)}), bf16[256,1024]{1,0:T(8,128)(2,1)}) %reduce-scatter.5.cloned.1.call-update) | async-done | bytes 524304 | tf_op jit(solution)/shard_map/reduce_scatter | solution.py:36
  454.8 1.2 fusion.74
  456.0 0.3 fusion.113
  456.3 1.9 dynamic-slice_multiply_fusion
  458.2 0.1 fusion.141
  458.4 0.8 pad_maximum_fusion
  459.1 6.6 convert_multiply_fusion.2
  465.7 25.8 %psum.28 = f32[1,5]{1,0:T(1,128)S(1)} all-reduce(f32[1,5]{1,0:T(1,128)S(1)} %pad_maximum_fusion), channel_id=1, replica_groups=mesh['section'=32,'tensor'=8] {'tensor'}, use_global_device_ids=true, to_apply=%region_6.7 | all-reduce | flops 5 | bytes 40 | tf_op jit(solution)/shard_map/psum | solution.py:42
  491.5 0.6 slice.38
  492.8 0.7 fusion.140
  505.7 0.2 fusion.116
  505.9 2.0 multiply_reduce_fusion
  507.9 74.5 %reduce-scatter.9.cloned.1.call-done = bf16[256,1024]{1,0:T(8,128)(2,1)} async-done(((bf16[256,8192]{1,0:T(8,128)(2,1)}), bf16[256,1024]{1,0:T(8,128)(2,1)}) %reduce-scatter.9.cloned.1.call-update) | async-done | bytes 524304 | tf_op jit(solution)/shard_map/reduce_scatter | solution.py:36
  582.4 1.6 fusion.68
  584.0 26.0 %all-reduce.4 = (f32[256]{0:T(256)S(1)}, f32[]{:T(128)}) all-reduce(f32[256]{0:T(256)S(1)} %fusion.68, f32[]{:T(128)} %multiply_reduce_fusion), channel_id=1, replica_groups=mesh['section'=32,'tensor'=8] {'tensor'}, use_global_device_ids=true, to_apply=%region_12.13 | all-reduce | flops 257 | bytes 2056 | tf_op jit(solution)/shard_map/psum | solution.py:42
  610.0 1.7 fusion.67
  611.7 1.9 collective-permute-start.1
  613.6 0.6 broadcast_divide_fusion.1
  614.3 1.9 subtract_multiply_fusion
  616.2 4.1 collective-permute-done.1
  620.3 0.8 copy-done.6
  621.1 1.0 fusion.76
  622.2 0.0 all-gather.11.cloned.1.call-start
  622.2 3.7 collective-permute-start
  625.9 7.0 collective-permute-done
  632.9 0.9 broadcast_select_fusion.1
  633.8 0.0 reduce-scatter.11.cloned.1.call-start
  633.8 54.6 %all-gather.21.cloned.1.call-done = bf16[1,256,8192]{2,1,0:T(8,128)(2,1)} async-done(((bf16[1,256,1024]{2,1,0:T(8,128)(2,1)}), bf16[1,256,8192]{2,1,0:T(8,128)(2,1)}) %all-gather.21.cloned.1.call-update) | async-done | bytes 4194320 | tf_op jit(solution)/shard_map/all_gather | solution.py:56
  688.4 3.3 fusion.7
  691.6 0.2 copy-done.1
  691.8 1.4 fusion.9
  693.2 104.2 %all-gather.13.cloned.1.call-done = bf16[256,8192]{1,0:T(8,128)(2,1)} async-done(((bf16[256,1024]{1,0:T(8,128)(2,1)}), bf16[256,8192]{1,0:T(8,128)(2,1)}) %all-gather.13.cloned.1.call-update) | async-done | bytes 4194320 | tf_op jit(solution)/shard_map/all_gather | solution.py:57
  797.5 9.3 convolution_convert_fusion
  806.8 0.3 reduce-scatter.7.cloned.1.call-start
  807.1 95.3 %all-gather.11.cloned.1.call-done = bf16[256,8192]{1,0:T(8,128)(2,1)} async-done(((bf16[256,1024]{1,0:T(8,128)(2,1)}), bf16[256,8192]{1,0:T(8,128)(2,1)}) %all-gather.11.cloned.1.call-update) | async-done | bytes 4194320 | tf_op jit(solution)/shard_map/all_gather | solution.py:32
  902.4 3.1 fusion
  905.5 8.0 convolution_convert_fusion.2
  913.5 6.6 convert_multiply_fusion
  920.1 108.4 %reduce-scatter.11.cloned.1.call-done = bf16[256,1024]{1,0:T(8,128)(2,1)} async-done(((bf16[256,8192]{1,0:T(8,128)(2,1)}), bf16[256,1024]{1,0:T(8,128)(2,1)}) %reduce-scatter.11.cloned.1.call-update) | async-done | bytes 524304 | tf_op jit(solution)/shard_map/reduce_scatter | solution.py:36
  1028.5 1.6 fusion.73
  1030.1 25.3 %psum.31 = f32[256]{0:T(256)S(1)} all-reduce(f32[256]{0:T(256)S(1)} %fusion.73), channel_id=1, replica_groups=mesh['section'=32,'tensor'=8] {'tensor'}, use_global_device_ids=true, to_apply=%region_16.17 | all-reduce | flops 256 | bytes 2048 | tf_op jit(solution)/shard_map/psum | solution.py:42
  1055.4 2.6 fusion.77
  1058.0 98.2 %reduce-scatter.7.cloned.1.call-done = bf16[256,1024]{1,0:T(8,128)(2,1)} async-done(((bf16[256,8192]{1,0:T(8,128)(2,1)}), bf16[256,1024]{1,0:T(8,128)(2,1)}) %reduce-scatter.7.cloned.1.call-update) | async-done | bytes 524304 | tf_op jit(solution)/shard_map/reduce_scatter | solution.py:36
  1156.3 2.0 fusion.75
  (44 shorter events, 0.4 us)
Async XLA Ops:
  7.2 116.6 %copy-start = (bf16[1,8192,128]{2,1,0:T(8,128)(2,1)S(1)}, bf16[1,8192,128]{2,1,0:T(8,128)(2,1)}, u32[]{:S(2)}) copy-start(bf16[1,8192,128]{2,1,0:T(8,128)(2,1)} %param.23) | copy-start | bytes 6291460
  7.2 116.6 %copy-start.10 = (f32[1,8192]{1,0:T(1,128)S(1)}, f32[1,8192]{1,0:T(1,128)}, u32[]{:S(2)}) copy-start(f32[1,8192]{1,0:T(1,128)} %param.22) | copy-start | bytes 98308
  7.2 113.5 %all-gather.15.cloned.1.call-start = ((), (), s32[]{:S(2)}) async-start(), calls=%async_computation.10 | async-start | bytes 4718592 | tf_op jit(solution)/shard_map/all_gather | solution.py:32
  7.9 217.1 %all-gather.17.cloned.1.call-start = ((), (), s32[]{:S(2)}) async-start(), calls=%async_computation.11 | async-start | bytes 4718592 | tf_op jit(solution)/shard_map/all_gather | solution.py:56
  8.7 320.7 %all-gather.19.cloned.1.call-start = ((), (), s32[]{:S(2)}) async-start(), calls=%async_computation.12 | async-start | bytes 4718592 | tf_op jit(solution)/shard_map/all_gather | solution.py:57
  9.4 445.4 %reduce-scatter.5.cloned.1.call-start = ((), (), s32[]{:S(2)}) async-start(), calls=%async_computation.4 | async-start | bytes 4718592 | tf_op jit(solution)/shard_map/reduce_scatter | solution.py:36
  131.2 97.1 %copy-start.9 = (f32[1,8192]{1,0:T(1,128)S(1)}, f32[1,8192]{1,0:T(1,128)}, u32[]{:S(2)}) copy-start(f32[1,8192]{1,0:T(1,128)} %param.25) | copy-start | bytes 98308
  131.2 451.1 %reduce-scatter.9.cloned.1.call-start = ((), (), s32[]{:S(2)}) async-start(), calls=%async_computation.7 | async-start | bytes 4718592 | tf_op jit(solution)/shard_map/reduce_scatter | solution.py:36
  225.0 3.4 copy-start.2
  339.3 1.2 copy-start.3
  339.3 1.5 copy-start.8
  339.3 3.0 copy-start.14
  339.3 6.2 copy-start.12
  339.3 118.9 %copy-start.11 = (f32[1024,4]{0,1:T(4,128)S(1)}, f32[1024,4]{0,1:T(4,128)}, u32[]{:S(2)}) copy-start(f32[1024,4]{0,1:T(4,128)} %param.29) | copy-start | bytes 49156
  339.3 349.0 %all-gather.21.cloned.1.call-start = ((), (), s32[]{:S(2)}) async-start(), calls=%async_computation.13 | async-start | bytes 4718592 | tf_op jit(solution)/shard_map/all_gather | solution.py:56
  341.6 455.8 %all-gather.13.cloned.1.call-start = ((), (), s32[]{:S(2)}) async-start(), calls=%async_computation.8 | async-start | bytes 4718592 | tf_op jit(solution)/shard_map/all_gather | solution.py:57
  459.1 33.7 %copy-start.13 = (f32[4]{0:T(128)S(1)}, f32[4]{0:T(128)}, u32[]{:S(2)}) copy-start(f32[4]{0:T(128)} %param.30) | copy-start | bytes 52
  459.1 150.8 %copy-start.5 = (bf16[1,256,1024]{2,1,0:T(8,128)(2,1)S(1)}, bf16[1,256,1024]{2,1,0:T(8,128)(2,1)}, u32[]{:S(2)}) copy-start(bf16[1,256,1024]{2,1,0:T(8,128)(2,1)} %param.20) | copy-start | bytes 1572868
  611.7 8.6 collective-permute-start.1
  620.3 0.8 copy-start.6
  622.2 280.2 %all-gather.11.cloned.1.call-start = ((), (), s32[]{:S(2)}) async-start(), calls=%async_computation.5 | async-start | bytes 4718592 | tf_op jit(solution)/shard_map/all_gather | solution.py:32
  622.2 10.7 collective-permute-start
  633.8 394.7 %reduce-scatter.11.cloned.1.call-start = ((), (), s32[]{:S(2)}) async-start(), calls=%async_computation.9 | async-start | bytes 4718592 | tf_op jit(solution)/shard_map/reduce_scatter | solution.py:36
  688.4 3.4 copy-start.1
  806.8 349.4 %reduce-scatter.7.cloned.1.call-start = ((), (), s32[]{:S(2)}) async-start(), calls=%async_computation.6 | async-start | bytes 4718592 | tf_op jit(solution)/shard_map/reduce_scatter | solution.py:36
  913.5 141.9 %copy-start.7 = (bf16[256,1024]{1,0:T(8,128)(2,1)S(1)}, bf16[256,1024]{1,0:T(8,128)(2,1)}, u32[]{:S(2)}) copy-start(bf16[256,1024]{1,0:T(8,128)(2,1)} %copy-done.6) | copy-start | bytes 1572868
  920.1 236.2 %copy-start.4 = (bf16[256,1024]{1,0:T(8,128)(2,1)S(1)}, bf16[256,1024]{1,0:T(8,128)(2,1)}, u32[]{:S(2)}) copy-start(bf16[256,1024]{1,0:T(8,128)(2,1)} %broadcast_select_fusion.1) | copy-start | bytes 1572868
Sparse Core Ops, SparseCore 0:
  10.7 109.9 all-gather.14
  123.3 101.6 all-gather.16
  227.7 101.6 all-gather.18
  333.4 121.3 reduce-scatter.4
  458.8 123.5 reduce-scatter.8
  585.4 102.8 all-gather.20
  691.0 106.4 all-gather.12
  800.7 101.6 all-gather.10
  906.6 121.8 reduce-scatter.10
  1032.5 123.7 reduce-scatter.6
where the time goes:
time: 1170 us
  waiting for transfers between devices  960 us (82%)
  blocking collectives  77.2 us (7%)
  other arithmetic  47.2 us (4%)
  matrix products  39.8 us (3%)
  between operations  30.4 us (3%)
    reduce_scatter x4, waiting for transfers between devices, reduce_columns(): lax.psum_scatter(partial_rows.astype(jnp.bfloat16), 'tensor', scatter_dim...  390 us
    all_gather x2, waiting for transfers between devices, gather_columns(): return lax.all_gather(local_rows, 'tensor', axis=1, tiled=True)  206 us
    all_gather x2, waiting for transfers between devices, layer_backward(): lax.all_gather(cotangent, 'tensor', axis=1, tiled=True)  202 us
    all_gather x2, waiting for transfers between devices, layer_backward(): lax.all_gather(saved_rows, 'tensor', axis=1, tiled=True)  148 us
    psum x3, blocking collectives, row_sums(): return lax.psum(values, 'tensor')  77.2 us
  transfers between devices with their start and end apart: 12, of which 12 were waited for; matrix products, arithmetic and copies ran while one was open for 7% of the time, Pallas kernels for 0%

commit v1 on v0

--- a/solution.py
+++ b/solution.py
@@ -29,7 +29,9 @@
 
 
 def gather_columns(local_rows):
-    return lax.all_gather(local_rows, "tensor", axis=1, tiled=True)
+    return jnp.concatenate(
+        lax.all_to_all(jnp.stack([local_rows] * lax.axis_size("tensor")), "tensor", 0, 0), axis=1
+    )
 
 
 def reduce_columns(partial_rows):

time: 1170 us -> 1100 us (0.940)
  waiting for transfers between devices: 960 us -> 863 us
  starting transfers between devices: 6.2 us -> 20.3 us
    all_gather x2 -> x0, waiting for transfers between devices: 206 us -> none  [gather_columns(): return lax.all_gather(local_rows, 'tensor', axis=1, tiled=True)]
    all_to_all x0 -> x2, waiting for transfers between devices: none -> 78.2 us  [gather_columns(): lax.all_to_all(jnp.stack([local_rows] * lax.axis_size('tensor')), 'tensor...]
    all_gather x2, waiting for transfers between devices: 202 us -> 255 us  [layer_backward(): lax.all_gather(cotangent, 'tensor', axis=1, tiled=True)]
    all_to_all x0 -> x2, starting transfers between devices: none -> 15.8 us  [gather_columns(): lax.all_to_all(jnp.stack([local_rows] * lax.axis_size('tensor')), 'tensor...]
    all_gather x2, waiting for transfers between devices: 148 us -> 135 us  [layer_backward(): lax.all_gather(saved_rows, 'tensor', axis=1, tiled=True)]
  transfers between devices with their start and end apart: 12 -> 12, of which waited for: 12 -> 11; matrix products, arithmetic and copies ran while one was open for 7% -> 9% of each run, Pallas kernels for 0% -> 0%
where the time goes in v1:
time: 1100 us
  waiting for transfers between devices  863 us (78%)
  blocking collectives  77.1 us (7%)
  other arithmetic  56.7 us (5%)
  matrix products  39.9 us (4%)
  between operations  29.9 us (3%)
  starting transfers between devices  20.3 us (2%)
    reduce_scatter x4, waiting for transfers between devices, reduce_columns(): lax.psum_scatter(partial_rows.astype(jnp.bfloat16), 'tensor', scatter_dim...  383 us
    all_gather x2, waiting for transfers between devices, layer_backward(): lax.all_gather(cotangent, 'tensor', axis=1, tiled=True)  255 us
    all_gather x2, waiting for transfers between devices, layer_backward(): lax.all_gather(saved_rows, 'tensor', axis=1, tiled=True)  135 us
    all_to_all x2, waiting for transfers between devices, gather_columns(): lax.all_to_all(jnp.stack([local_rows] * lax.axis_size('tensor')), 'tensor...  78.2 us
    psum x3, blocking collectives, row_sums(): return lax.psum(values, 'tensor')  77.1 us
  transfers between devices with their start and end apart: 12, of which 11 were waited for; matrix products, arithmetic and copies ran while one was open for 9% of the time, Pallas kernels for 0%

profile of v1, /device:TPU:2, one launch (start us, length us, event | category | flops | bytes accessed | tf_op | source)
XLA Modules:
  0.0 1098.1 jit_solution(3362236316368695256)
XLA Ops:
  7.2 0.7 all-gather.11.cloned.1.call-update
  7.9 1.2 copy.19
  9.2 2.2 stack.4
  11.4 11.2 %all-to-all-start = ((bf16[8,256,1024]{1,2,0:T(8,128)(2,1)}), bf16[8,256,1024]{1,2,0:T(8,128)(2,1)}, u32[]{:S(2)}, u32[]{:S(2)}) async-start(bf16[8,256,1024]{1,2,0:T(8,128)(2,1)} %stack.4), calls=%async_computation | async-start | bytes 8388608 | tf_op jit(solution)/shard_map/all_to_all | solution.py:33
  22.7 0.7 all-gather.13.cloned.1.call-update
  23.4 0.6 broadcast.173
  24.0 0.7 reduce.15
  24.8 78.2 %all-to-all-done = bf16[8,256,1024]{1,2,0:T(8,128)(2,1)} async-done(((bf16[8,256,1024]{1,2,0:T(8,128)(2,1)}), bf16[8,256,1024]{1,2,0:T(8,128)(2,1)}, u32[]{:S(2)}, u32[]{:S(2)}) %all-to-all-start) | async-done | bytes 4194336 | tf_op jit(solution)/shard_map/all_to_all | solution.py:33
  103.0 3.3 fusion
  106.3 4.2 fusion.2
  110.5 7.3 convolution_convert_fusion.3
  117.8 68.3 %all-gather.11.cloned.1.call-done = bf16[1,256,8192]{2,1,0:T(8,128)(2,1)} async-done(((bf16[1,256,1024]{2,1,0:T(8,128)(2,1)}), bf16[1,256,8192]{2,1,0:T(8,128)(2,1)}) %all-gather.11.cloned.1.call-update) | async-done | bytes 4194320 | tf_op jit(solution)/shard_map/all_gather | solution.py:58
  186.2 3.3 fusion.7
  189.6 3.0 fusion.8
  192.6 101.0 %all-gather.13.cloned.1.call-done = bf16[1,256,8192]{2,1,0:T(8,128)(2,1)} async-done(((bf16[1,256,1024]{2,1,0:T(8,128)(2,1)}), bf16[1,256,8192]{2,1,0:T(8,128)(2,1)}) %all-gather.13.cloned.1.call-update) | async-done | bytes 4194320 | tf_op jit(solution)/shard_map/all_gather | solution.py:59
  293.6 9.9 convolution_convert_fusion.1
  303.7 1.0 copy-done.3
  304.7 0.3 copy-done.7
  305.0 0.8 bitcast_select_fusion
  305.9 0.2 all-gather.9.cloned.1.call-start
  306.8 0.7 fusion.123
  310.0 0.6 fusion.121
  310.6 109.1 %reduce-scatter.5.cloned.1.call-done = bf16[256,1024]{1,0:T(8,128)(2,1)} async-done(((bf16[256,8192]{1,0:T(8,128)(2,1)}), bf16[256,1024]{1,0:T(8,128)(2,1)}) %reduce-scatter.5.cloned.1.call-update) | async-done | bytes 524304 | tf_op jit(solution)/shard_map/reduce_scatter | solution.py:38
  419.7 1.2 add_convert_fusion.1
  420.9 0.3 fusion.97
  421.2 1.9 dynamic-slice_multiply_fusion
  423.3 0.8 pad_maximum_fusion
  424.1 6.6 convert_multiply_fusion
  430.6 25.7 %psum.28 = f32[1,5]{1,0:T(1,128)S(1)} all-reduce(f32[1,5]{1,0:T(1,128)S(1)} %pad_maximum_fusion), channel_id=1, replica_groups=mesh['section'=32,'tensor'=8] {'tensor'}, use_global_device_ids=true, to_apply=%region_6.7 | all-reduce | flops 5 | bytes 40 | tf_op jit(solution)/shard_map/psum | solution.py:44
  456.3 0.6 slice.38
  457.6 0.7 fusion.124
  470.0 0.2 fusion.100
  470.2 2.0 multiply_reduce_fusion
  472.2 74.5 %reduce-scatter.9.cloned.1.call-done = bf16[256,1024]{1,0:T(8,128)(2,1)} async-done(((bf16[256,8192]{1,0:T(8,128)(2,1)}), bf16[256,1024]{1,0:T(8,128)(2,1)}) %reduce-scatter.9.cloned.1.call-update) | async-done | bytes 524304 | tf_op jit(solution)/shard_map/reduce_scatter | solution.py:38
  546.7 1.6 fusion.61
  548.3 26.0 %all-reduce.4 = (f32[256]{0:T(256)S(1)}, f32[]{:T(128)}) all-reduce(f32[256]{0:T(256)S(1)} %fusion.61, f32[]{:T(128)} %multiply_reduce_fusion), channel_id=1, replica_groups=mesh['section'=32,'tensor'=8] {'tensor'}, use_global_device_ids=true, to_apply=%region_12.13 | all-reduce | flops 257 | bytes 2056 | tf_op jit(solution)/shard_map/psum | solution.py:44
  574.3 1.7 fusion.60
  576.1 1.9 collective-permute-start.1
  578.0 0.6 broadcast_divide_fusion.1
  578.6 2.0 subtract_multiply_fusion
  580.6 4.1 collective-permute-done.1
  584.7 0.8 copy-done.5
  585.5 1.0 fusion.68
  586.5 66.2 %all-gather.7.cloned.1.call-done = bf16[256,8192]{1,0:T(8,128)(2,1)} async-done(((bf16[256,1024]{1,0:T(8,128)(2,1)}), bf16[256,8192]{1,0:T(8,128)(2,1)}) %all-gather.7.cloned.1.call-update) | async-done | bytes 4194320 | tf_op jit(solution)/shard_map/all_gather | solution.py:58
  652.7 3.3 fusion.6
  656.0 1.9 collective-permute-start
  657.9 1.4 fusion.9
  659.3 7.1 collective-permute-done
  666.7 2.2 stack.5
  669.0 4.5 all-to-all-start.1
  673.6 153.6 %all-gather.9.cloned.1.call-done = bf16[256,8192]{1,0:T(8,128)(2,1)} async-done(((bf16[256,1024]{1,0:T(8,128)(2,1)}), bf16[256,8192]{1,0:T(8,128)(2,1)}) %all-gather.9.cloned.1.call-update) | async-done | bytes 4194320 | tf_op jit(solution)/shard_map/all_gather | solution.py:59
  827.2 9.4 convolution_convert_fusion
  836.6 0.3 reduce-scatter.7.cloned.1.call-start
  836.9 0.7 reduce.16
  837.6 3.3 fusion.3
  840.9 4.2 fusion.5
  845.1 8.2 convolution_convert_fusion.2
  853.4 6.6 convert_multiply_fusion.2
  860.0 101.4 %reduce-scatter.11.cloned.1.call-done = bf16[256,1024]{1,0:T(8,128)(2,1)} async-done(((bf16[256,8192]{1,0:T(8,128)(2,1)}), bf16[256,1024]{1,0:T(8,128)(2,1)}) %reduce-scatter.11.cloned.1.call-update) | async-done | bytes 524304 | tf_op jit(solution)/shard_map/reduce_scatter | solution.py:38
  961.4 1.6 fusion.66
  963.0 25.4 %psum.31 = f32[256]{0:T(256)S(1)} all-reduce(f32[256]{0:T(256)S(1)} %fusion.66), channel_id=1, replica_groups=mesh['section'=32,'tensor'=8] {'tensor'}, use_global_device_ids=true, to_apply=%region_16.17 | all-reduce | flops 256 | bytes 2048 | tf_op jit(solution)/shard_map/psum | solution.py:44
  988.4 2.6 fusion.69
  991.0 98.2 %reduce-scatter.7.cloned.1.call-done = bf16[256,1024]{1,0:T(8,128)(2,1)} async-done(((bf16[256,8192]{1,0:T(8,128)(2,1)}), bf16[256,1024]{1,0:T(8,128)(2,1)}) %reduce-scatter.7.cloned.1.call-update) | async-done | bytes 524304 | tf_op jit(solution)/shard_map/reduce_scatter | solution.py:38
  1089.2 2.0 fusion.67
  (53 shorter events, 1.1 us)
Async XLA Ops:
  7.2 103.3 %copy-start = (bf16[1,8192,128]{2,1,0:T(8,128)(2,1)S(1)}, bf16[1,8192,128]{2,1,0:T(8,128)(2,1)}, u32[]{:S(2)}) copy-start(bf16[1,8192,128]{2,1,0:T(8,128)(2,1)} %param.23) | copy-start | bytes 6291460
  7.2 179.0 %all-gather.11.cloned.1.call-start = ((), (), s32[]{:S(2)}) async-start(), calls=%async_computation.12 | async-start | bytes 4718592 | tf_op jit(solution)/shard_map/all_gather | solution.py:58
  11.4 12.6 %copy-start.10 = (f32[1,8192]{1,0:T(1,128)S(1)}, f32[1,8192]{1,0:T(1,128)}, u32[]{:S(2)}) copy-start(f32[1,8192]{1,0:T(1,128)} %param.22) | copy-start | bytes 98308
  11.4 91.6 %all-to-all-start = ((bf16[8,256,1024]{1,2,0:T(8,128)(2,1)}), bf16[8,256,1024]{1,2,0:T(8,128)(2,1)}, u32[]{:S(2)}, u32[]{:S(2)}) async-start(bf16[8,256,1024]{1,2,0:T(8,128)(2,1)} %stack.4), calls=%async_computation | async-start | bytes 8388608 | tf_op jit(solution)/shard_map/all_to_all | solution.py:33
  22.6 271.0 %all-gather.13.cloned.1.call-start = ((), (), s32[]{:S(2)}) async-start(), calls=%async_computation.13 | async-start | bytes 4718592 | tf_op jit(solution)/shard_map/all_gather | solution.py:59
  23.4 396.3 %reduce-scatter.5.cloned.1.call-start = ((), (), s32[]{:S(2)}) async-start(), calls=%async_computation.6 | async-start | bytes 4718592 | tf_op jit(solution)/shard_map/reduce_scatter | solution.py:38
  117.8 71.7 %copy-start.9 = (f32[1,8192]{1,0:T(1,128)S(1)}, f32[1,8192]{1,0:T(1,128)}, u32[]{:S(2)}) copy-start(f32[1,8192]{1,0:T(1,128)} %param.25) | copy-start | bytes 98308
  117.8 428.9 %reduce-scatter.9.cloned.1.call-start = ((), (), s32[]{:S(2)}) async-start(), calls=%async_computation.8 | async-start | bytes 4718592 | tf_op jit(solution)/shard_map/reduce_scatter | solution.py:38
  186.2 3.4 copy-start.2
  303.6 1.1 copy-start.3
  303.6 1.5 copy-start.7
  303.6 3.2 copy-start.14
  303.6 6.4 copy-start.12
  303.6 119.6 %copy-start.11 = (f32[1024,4]{0,1:T(4,128)S(1)}, f32[1024,4]{0,1:T(4,128)}, u32[]{:S(2)}) copy-start(f32[1024,4]{0,1:T(4,128)} %param.29) | copy-start | bytes 49156
  303.6 349.1 %all-gather.7.cloned.1.call-start = ((), (), s32[]{:S(2)}) async-start(), calls=%async_computation.9 | async-start | bytes 4718592 | tf_op jit(solution)/shard_map/all_gather | solution.py:58
  305.9 521.3 %all-gather.9.cloned.1.call-start = ((), (), s32[]{:S(2)}) async-start(), calls=%async_computation.10 | async-start | bytes 4718592 | tf_op jit(solution)/shard_map/all_gather | solution.py:59
  424.1 33.6 %copy-start.13 = (f32[4]{0:T(128)S(1)}, f32[4]{0:T(128)}, u32[]{:S(2)}) copy-start(f32[4]{0:T(128)} %param.30) | copy-start | bytes 52
  424.1 150.3 %copy-start.4 = (bf16[1,256,1024]{2,1,0:T(8,128)(2,1)S(1)}, bf16[1,256,1024]{2,1,0:T(8,128)(2,1)}, u32[]{:S(2)}) copy-start(bf16[1,256,1024]{2,1,0:T(8,128)(2,1)} %param.20) | copy-start | bytes 1572868
  576.1 8.6 collective-permute-start.1
  584.7 0.8 copy-start.5
  652.7 5.2 copy-start.1
  656.0 10.5 collective-permute-start
  657.9 8.6 copy-start.8
  669.0 168.6 %all-to-all-start.1 = ((bf16[8,256,1024]{1,2,0:T(8,128)(2,1)}), bf16[8,256,1024]{1,2,0:T(8,128)(2,1)}, u32[]{:S(2)}, u32[]{:S(2)}) async-start(bf16[8,256,1024]{1,2,0:T(8,128)(2,1)} %stack.5), calls=%async_computation.2 | async-start | bytes 8388608 | tf_op jit(solution)/shard_map/all_to_all | solution.py:33
  673.5 287.9 %reduce-scatter.11.cloned.1.call-start = ((), (), s32[]{:S(2)}) async-start(), calls=%async_computation.11 | async-start | bytes 4718592 | tf_op jit(solution)/shard_map/reduce_scatter | solution.py:38
  836.6 252.6 %reduce-scatter.7.cloned.1.call-start = ((), (), s32[]{:S(2)}) async-start(), calls=%async_computation.7 | async-start | bytes 4718592 | tf_op jit(solution)/shard_map/reduce_scatter | solution.py:38
  853.4 135.0 %copy-start.6 = (bf16[256,1024]{1,0:T(8,128)(2,1)S(1)}, bf16[256,1024]{1,0:T(8,128)(2,1)}, u32[]{:S(2)}) copy-start(bf16[256,1024]{1,0:T(8,128)(2,1)} %copy-done.5) | copy-start | bytes 1572868
Sparse Core Ops, SparseCore 0:
  10.7 175.4 all-gather.10
  188.8 104.7 all-gather.12
  297.8 121.8 reduce-scatter.4
  423.7 122.9 reduce-scatter.8
  549.8 102.8 all-gather.6
  655.8 171.3 all-gather.8
  836.7 124.6 reduce-scatter.10
  965.6 123.6 reduce-scatter.6
